TPU v7x, 32 devices: a whole 2x2x4 slice. The times are simulated.
32 devices in a mesh: dp: 8 (over y, x, core), tensor: 4 (over z).
Axes of the slice: x: 2, y: 2, z: 4, core: 2. Of those that a mesh axis runs over, the one named last changes fastest.
Arguments:
- inputs: bfloat16 [768, 32768], P('tensor', 'dp'), may hold values from -18 to 18
- cotangent: float32 [768, 32768], P('tensor', 'dp'), may hold values from -18 to 18
- query_w: bfloat16 [768, 192], P('tensor'), may hold values from -0.21875 to 0.21875
- key_w: bfloat16 [768, 192], P('tensor'), may hold values from -0.21875 to 0.21875
- value_w: bfloat16 [768, 192], P('tensor'), may hold values from -0.4375 to 0.4375
- query_b: float32 [768], P('tensor'), may hold values from -1.75 to 1.75
- value_b: float32 [768], P('tensor'), may hold values from -0.0625 to 0.0625
- output_w: bfloat16 [768, 768], P(None, 'tensor'), may hold values from -4 to 4
- output_b: float32 [768], P('tensor'), may hold values from -1.25 to 1.25
- first_gain: float32 [768], P('tensor'), may hold values from 0.5 to 1.5
- first_shift: float32 [768], P('tensor'), may hold values from -1.25 to 1.25
- inner_w: bfloat16 [3072, 192], P('tensor'), may hold values from -0.4375 to 0.4375
- inner_b: float32 [3072], P('tensor'), may hold values from -1.25 to 1.25
- outer_w: bfloat16 [768, 768], P('tensor'), may hold values from -0.21875 to 0.21875
- outer_b: float32 [768], P('tensor'), may hold values from -1.25 to 1.25
- second_gain: float32 [768], P('tensor'), may hold values from 0.5 to 1.5
- second_shift: float32 [768], P('tensor'), may hold values from -1.25 to 1.25
Outputs:
- layer_out: bfloat16 [768, 32768], P('tensor', 'dp')
- input_grad: bfloat16 [768, 32768], P('tensor', 'dp')
- grad_query_w: float32 [768, 192], P('tensor')
- grad_key_w: float32 [768, 192], P('tensor')
- grad_value_w: float32 [768, 192], P('tensor')
- grad_query_b: float32 [768], P('tensor')
- grad_value_b: float32 [768], P('tensor')
- grad_output_w: float32 [768, 768], P(None, 'tensor')
- grad_output_b: float32 [768], P('tensor')
- grad_first_gain: float32 [768], P('tensor')
- grad_first_shift: float32 [768], P('tensor')
- grad_inner_w: float32 [3072, 192], P('tensor')
- grad_inner_b: float32 [3072], P('tensor')
- grad_outer_w: float32 [768, 768], P('tensor')
- grad_outer_b: float32 [768], P('tensor')
- grad_second_gain: float32 [768], P('tensor')
- grad_second_shift: float32 [768], P('tensor')
All inputs are finite; a program needn't handle non-finite values.
Results may differ from a plain program's by a relative error of at most 0.0095.
Values may be sent and summed in bfloat16 or wider, within the bound.
No kernel may reach another device: no remote copies, remote signals or barrier semaphores. Data moves between devices by JAX's collectives and lax.ppermute only.
A program may use at most 128 MiB of HBM per device.

v0:
```python
from functools import partial

import jax
import jax.numpy as jnp
from jax import lax
from jax.sharding import PartitionSpec as P

D = 768
HDIM = 64
SEQ_LEN = 1024
QBLOCK = 512


EPSILON = 1e-05


def contract_tokens(left, right):
    return lax.dot_general(
        left, right, (((1,), (1,)), ((), ())), preferred_element_type=jnp.float32
    )


def through_weight(weight, grad):
    return lax.dot_general(
        weight, grad, (((0,), (0,)), ((), ())), preferred_element_type=jnp.float32
    )


def per_sequence(array, heads_here):
    number = array.shape[1] // SEQ_LEN
    return jnp.moveaxis(array.reshape(heads_here, HDIM, number, SEQ_LEN), 2, 0)


def to_channels(array):
    number, heads_here = (array.shape[0], array.shape[1])
    return jnp.moveaxis(array, 0, 2).reshape(heads_here * HDIM, number * SEQ_LEN)


def by_blocks(array):
    return jnp.moveaxis(
        array.reshape(array.shape[0], array.shape[1], SEQ_LEN // QBLOCK, QBLOCK), 2, 0
    )


def from_blocks(array):
    return jnp.moveaxis(array, 0, 2).reshape(array.shape[1], array.shape[2], SEQ_LEN)


def attend_forward(triple):
    query, keys, values = triple
    scale = HDIM ** (-0.5)

    def one_block(query_part):
        scores = (
            jnp.einsum("hdq,hdk->hqk", query_part, keys, preferred_element_type=jnp.float32) * scale
        )
        highest = jnp.max(scores, axis=-1, keepdims=True)
        expo = jnp.exp(scores - highest)
        totals = jnp.sum(expo, axis=-1, keepdims=True)
        probs_low = (expo / totals).astype(jnp.bfloat16)
        context = jnp.einsum("hqk,hdk->hdq", probs_low, values, preferred_element_type=jnp.float32)
        return (context, jnp.swapaxes(highest, 1, 2), jnp.swapaxes(totals, 1, 2))

    context, highest, totals = lax.map(one_block, by_blocks(query))
    return (from_blocks(context), from_blocks(highest), from_blocks(totals))


def attend_backward(sextet):
    query, keys, values, grad_context, highest, totals = sextet
    scale = HDIM ** (-0.5)

    def one_block(carry, block):
        grad_keys, grad_values = carry
        query_part, grad_part, high_part, total_part = block
        scores = (
            jnp.einsum("hdq,hdk->hqk", query_part, keys, preferred_element_type=jnp.float32) * scale
        )
        probs = jnp.exp(scores - jnp.swapaxes(high_part, 1, 2)) / jnp.swapaxes(total_part, 1, 2)
        probs_low = probs.astype(jnp.bfloat16)
        grad_probs = jnp.einsum(
            "hdq,hdk->hqk", grad_part, values, preferred_element_type=jnp.float32
        )
        inner_sum = jnp.sum(probs * grad_probs, axis=-1, keepdims=True)
        grad_scores = (probs * (grad_probs - inner_sum)).astype(jnp.bfloat16)
        grad_query = (
            jnp.einsum("hqk,hdk->hdq", grad_scores, keys, preferred_element_type=jnp.float32)
            * scale
        )
        grad_keys = (
            grad_keys
            + jnp.einsum(
                "hqk,hdq->hdk", grad_scores, query_part, preferred_element_type=jnp.float32
            )
            * scale
        )
        grad_values = grad_values + jnp.einsum(
            "hqk,hdq->hdk", probs_low, grad_part, preferred_element_type=jnp.float32
        )
        return ((grad_keys, grad_values), grad_query)

    zeros = jnp.zeros(keys.shape, jnp.float32)
    (grad_keys, grad_values), grad_query = lax.scan(
        one_block,
        (zeros, zeros),
        (by_blocks(query), by_blocks(grad_context), by_blocks(highest), by_blocks(totals)),
    )
    return (from_blocks(grad_query), grad_keys, grad_values)


def norm_backward(grad_hidden, gain, normed, inv_std, sums):
    scaled = grad_hidden * gain[:, None]
    return inv_std * (scaled - sums[0] / D - normed * (sums[1] / D))


def shards(
    inputs,
    cotangent,
    query_w,
    key_w,
    value_w,
    query_b,
    value_b,
    output_w,
    output_b,
    first_gain,
    first_shift,
    inner_w,
    inner_b,
    outer_w,
    outer_b,
    second_gain,
    second_shift,
):
    local = inputs.shape[0]
    tokens = inputs.shape[1]
    heads_here = local // HDIM
    query = (
        jnp.dot(query_w, inputs, preferred_element_type=jnp.float32) + query_b[:, None]
    ).astype(jnp.bfloat16)
    keys = jnp.dot(key_w, inputs, preferred_element_type=jnp.float32).astype(jnp.bfloat16)
    values = (
        jnp.dot(value_w, inputs, preferred_element_type=jnp.float32) + value_b[:, None]
    ).astype(jnp.bfloat16)
    query_seq = per_sequence(query, heads_here)
    keys_seq = per_sequence(keys, heads_here)
    values_seq = per_sequence(values, heads_here)
    context, highest, totals = lax.map(attend_forward, (query_seq, keys_seq, values_seq))
    context_low = to_channels(context).astype(jnp.bfloat16)
    attended = lax.psum_scatter(
        jnp.dot(output_w, context_low, preferred_element_type=jnp.float32),
        "tensor",
        scatter_dimension=0,
        tiled=True,
    )
    first_resid = inputs.astype(jnp.float32) + attended + output_b[:, None]
    first_center = lax.psum(jnp.sum(first_resid, axis=0), "tensor") / D
    first_offset = first_resid - first_center
    first_spread = lax.psum(jnp.sum(first_offset * first_offset, axis=0), "tensor") / D
    first_inv = lax.rsqrt(first_spread + EPSILON)
    first_normed = first_offset * first_inv
    first_hidden = first_normed * first_gain[:, None] + first_shift[:, None]
    hidden_low = first_hidden.astype(jnp.bfloat16)
    inner = jnp.dot(inner_w, hidden_low, preferred_element_type=jnp.float32) + inner_b[:, None]
    activ, gelu_pull = jax.vjp(partial(jax.nn.gelu, approximate=False), inner)
    act_low = activ.astype(jnp.bfloat16)
    second_resid = (
        first_hidden
        + jnp.dot(outer_w, act_low, preferred_element_type=jnp.float32)
        + outer_b[:, None]
    )
    second_center = lax.psum(jnp.sum(second_resid, axis=0), "tensor") / D
    second_offset = second_resid - second_center
    second_spread = lax.psum(jnp.sum(second_offset * second_offset, axis=0), "tensor") / D
    second_inv = lax.rsqrt(second_spread + EPSILON)
    second_normed = second_offset * second_inv
    layer_out = (second_normed * second_gain[:, None] + second_shift[:, None]).astype(jnp.bfloat16)
    grad_second_gain = jnp.sum(cotangent * second_normed, axis=1)
    grad_second_shift = jnp.sum(cotangent, axis=1)
    second_scaled = cotangent * second_gain[:, None]
    second_sums_back = (
        lax.psum(jnp.sum(second_scaled, axis=0).astype(jnp.bfloat16), "tensor").astype(jnp.float32),
        lax.psum(
            jnp.sum(second_scaled * second_normed, axis=0).astype(jnp.bfloat16), "tensor"
        ).astype(jnp.float32),
    )
    grad_second_resid = norm_backward(
        cotangent, second_gain, second_normed, second_inv, second_sums_back
    )
    outer_grad_low = grad_second_resid.astype(jnp.bfloat16)
    grad_outer_b = jnp.sum(outer_grad_low.astype(jnp.float32), axis=1)
    grad_outer_w = contract_tokens(outer_grad_low, act_low)
    grad_act = through_weight(outer_w, outer_grad_low)
    inner_grad_low = gelu_pull(grad_act)[0].astype(jnp.bfloat16)
    grad_inner_b = jnp.sum(inner_grad_low.astype(jnp.float32), axis=1)
    grad_inner_w = contract_tokens(inner_grad_low, hidden_low)
    grad_first_hidden = grad_second_resid + through_weight(inner_w, inner_grad_low)
    grad_first_gain = jnp.sum(grad_first_hidden * first_normed, axis=1)
    grad_first_shift = jnp.sum(grad_first_hidden, axis=1)
    first_scaled = grad_first_hidden * first_gain[:, None]
    first_sums_back = (
        lax.psum(jnp.sum(first_scaled, axis=0).astype(jnp.bfloat16), "tensor").astype(jnp.float32),
        lax.psum(
            jnp.sum(first_scaled * first_normed, axis=0).astype(jnp.bfloat16), "tensor"
        ).astype(jnp.float32),
    )
    grad_first_resid = norm_backward(
        grad_first_hidden, first_gain, first_normed, first_inv, first_sums_back
    )
    attended_grad_low = grad_first_resid.astype(jnp.bfloat16)
    grad_output_b = jnp.sum(attended_grad_low.astype(jnp.float32), axis=1)
    piece = lax.all_gather(attended_grad_low, "tensor", axis=0, tiled=True)
    start = jnp.int32(0)
    weight_rows = lax.dynamic_slice_in_dim(output_w, start, piece.shape[0], 0)
    grad_ctx = jnp.zeros((local, tokens), jnp.float32) + through_weight(weight_rows, piece)
    grad_weight = lax.dynamic_update_slice_in_dim(
        jnp.zeros(output_w.shape, jnp.float32), contract_tokens(piece, context_low), start, 0
    )
    context_grad_low = per_sequence(grad_ctx.astype(jnp.bfloat16), heads_here)
    grad_query, grad_keys, grad_values = lax.map(
        attend_backward, (query_seq, keys_seq, values_seq, context_grad_low, highest, totals)
    )
    query_grad_low = to_channels(grad_query).astype(jnp.bfloat16)
    keys_grad_low = to_channels(grad_keys).astype(jnp.bfloat16)
    values_grad_low = to_channels(grad_values).astype(jnp.bfloat16)
    grad_query_w = contract_tokens(query_grad_low, inputs)
    grad_key_w = contract_tokens(keys_grad_low, inputs)
    grad_value_w = contract_tokens(values_grad_low, inputs)
    grad_query_b = jnp.sum(query_grad_low.astype(jnp.float32), axis=1)
    grad_value_b = jnp.sum(values_grad_low.astype(jnp.float32), axis=1)
    input_grad = (
        grad_first_resid
        + through_weight(query_w, query_grad_low)
        + through_weight(key_w, keys_grad_low)
        + through_weight(value_w, values_grad_low)
    ).astype(jnp.bfloat16)
    summed = lax.psum(
        (
            grad_query_w,
            grad_key_w,
            grad_value_w,
            grad_query_b,
            grad_value_b,
            grad_weight,
            grad_output_b,
            grad_first_gain,
            grad_first_shift,
            grad_inner_w,
            grad_inner_b,
            grad_outer_w,
            grad_outer_b,
            grad_second_gain,
            grad_second_shift,
        ),
        "dp",
    )
    return (
        layer_out,
        input_grad,
        summed[0],
        summed[1],
        summed[2],
        summed[3],
        summed[4],
        summed[5],
        summed[6],
        summed[7],
        summed[8],
        summed[9],
        summed[10],
        summed[11],
        summed[12],
        summed[13],
        summed[14],
    )


def solution(mesh):
    placed = (
        P("tensor", "dp"),
        P("tensor", "dp"),
        P("tensor", None),
        P("tensor", None),
        P("tensor", None),
        P("tensor"),
        P("tensor"),
        P(None, "tensor"),
        P("tensor"),
        P("tensor"),
        P("tensor"),
        P("tensor", None),
        P("tensor"),
        P("tensor", None),
        P("tensor"),
        P("tensor"),
        P("tensor"),
    )
    return jax.shard_map(
        shards,
        mesh=mesh,
        in_specs=placed,
        out_specs=(
            P("tensor", "dp"),
            P("tensor", "dp"),
            P("tensor", None),
            P("tensor", None),
            P("tensor", None),
            P("tensor"),
            P("tensor"),
            P(None, "tensor"),
            P("tensor"),
            P("tensor"),
            P("tensor"),
            P("tensor", None),
            P("tensor"),
            P("tensor", None),
            P("tensor"),
            P("tensor"),
            P("tensor"),
        ),
        check_vma=False,
    )
```

profile of v0, /device:TPU:0, one launch (start us, length us, event | category | flops | bytes accessed | tf_op | source)
XLA Modules:
  0.0 836.4 jit_solution(991804344389069406)
XLA Ops:
  21.0 4.1 copy_bitcast_fusion.3
  25.3 53.3 %while.58 = (s32[]{:T(128)}, bf16[4,3,64,1024]{3,2,1,0:T(8,128)(2,1)S(1)}, f32[4,3,1,1024]{3,2,1,0:T(1,128)}, f32[4,3,1,1024]{3,2,1,0:T(1,128)}, bf16[4,3,64,102...) while((s32[]{:T(128)}, ...), condition=%wide.region_5.6_spmd, body=%wide.region_0.5_spmd.sunk | while | flops 416805888 | bytes 26757424 | solution.py:147
  27.9 8.6 %while.61 = (s32[]{:T(128)}, bf16[2,3,64,512]{3,2,1,0:T(8,128)(2,1)S(1)}, f32[2,3,1,512]{3,1,2,0:T(4,128)S(1)}, f32[2,3,1,512]{3,1,2,0:T(4,128)S(1)}, bf16[2,3,6...) while((s32[]{:T(128)}, ...), condition=%wide.region_4.4_spmd, body=%wide.region_1.3_spmd.sunk | while | flops 416805888 | bytes 20318312 | solution.py:64
  41.1 8.6 %while.61 = (s32[]{:T(128)}, bf16[2,3,64,512]{3,2,1,0:T(8,128)(2,1)S(1)}, f32[2,3,1,512]{3,1,2,0:T(4,128)S(1)}, f32[2,3,1,512]{3,1,2,0:T(4,128)S(1)}, bf16[2,3,6...) while((s32[]{:T(128)}, ...), condition=%wide.region_4.4_spmd, body=%wide.region_1.3_spmd.sunk | while | flops 416805888 | bytes 20318312 | solution.py:64
  54.3 8.6 %while.61 = (s32[]{:T(128)}, bf16[2,3,64,512]{3,2,1,0:T(8,128)(2,1)S(1)}, f32[2,3,1,512]{3,1,2,0:T(4,128)S(1)}, f32[2,3,1,512]{3,1,2,0:T(4,128)S(1)}, bf16[2,3,6...) while((s32[]{:T(128)}, ...), condition=%wide.region_4.4_spmd, body=%wide.region_1.3_spmd.sunk | while | flops 416805888 | bytes 20318312 | solution.py:64
  67.5 8.6 %while.61 = (s32[]{:T(128)}, bf16[2,3,64,512]{3,2,1,0:T(8,128)(2,1)S(1)}, f32[2,3,1,512]{3,1,2,0:T(4,128)S(1)}, f32[2,3,1,512]{3,1,2,0:T(4,128)S(1)}, bf16[2,3,6...) while((s32[]{:T(128)}, ...), condition=%wide.region_4.4_spmd, body=%wide.region_1.3_spmd.sunk | while | flops 416805888 | bytes 20318312 | solution.py:64
  81.6 6.3 convolution_bitcast_fusion
  88.0 12.7 %copy.101 = f32[768,4096]{1,0:T(8,128)} copy(f32[768,4096]{0,1:T(8,128)} %convolution_bitcast_fusion) | data formatting | bytes 25165824
  100.8 214.7 %reduce-scatter.4.cloned.1.call-done = f32[192,4096]{1,0:T(8,128)} async-done(((f32[768,4096]{1,0:T(8,128)}), f32[192,4096]{1,0:T(8,128)}) %reduce-scatter.4.cloned.1.call-update) | async-done | bytes 3145744 | tf_op jit(solution)/shard_map/reduce_scatter | solution.py:149
  318.4 18.6 %psum.161 = f32[4096]{0:T(1024)S(1)} all-reduce(f32[4096]{0:T(1024)S(1)} %get-tuple-element.431), channel_id=1, replica_groups=mesh['dp'=8,'tensor'=4] {'tensor'}, use_global_device_ids=true, to_apply=%region_8.9 | all-reduce | flops 4096 | bytes 32768 | tf_op jit(solution)/shard_map/psum | solution.py:156
  337.4 15.5 %psum.162 = f32[4096]{0:T(1024)S(1)} all-reduce(f32[4096]{0:T(1024)S(1)} %multiply_reduce_fusion.7), channel_id=1, replica_groups=mesh['dp'=8,'tensor'=4] {'tensor'}, use_global_device_ids=true, to_apply=%region_10.11 | all-reduce | flops 4096 | bytes 32768 | tf_op jit(solution)/shard_map/psum | solution.py:158
  353.1 31.2 %fusion.39 = (bf16[768,4096]{0,1:T(8,128)(2,1)S(1)}, f32[768,4096]{0,1:T(8,128)}, f32[4096,768]{1,0:T(8,128)}) fusion(f32[768]{0:T(1024)S(1)} %copy-done.53, bf16[768,192]{0,1:T(8,128)(2,1)S(1)} %copy-done, f32[192,4096]{1,0:T(8,128)S(1)} %get-tuple-element.432, f32[192]{0:T(256)S(1)} %copy-done.55, f32[192]{0:T(256)S(1)} %copy-done.38, ...), kind=kOutput, calls=%fused_computation.74 | convolution fusion | flops 1419509760 | bytes 34935296 | tf_op jit(solution)/shard_map/dot_general | solution.py:163
  388.3 16.4 %psum.163 = f32[4096]{0:T(1024)S(1)} all-reduce(f32[4096]{0:T(1024)S(1)} %get-tuple-element.447), channel_id=1, replica_groups=mesh['dp'=8,'tensor'=4] {'tensor'}, use_global_device_ids=true, to_apply=%region_12.13 | all-reduce | flops 4096 | bytes 32768 | tf_op jit(solution)/shard_map/psum | solution.py:171
  407.0 15.8 %psum.164 = f32[4096]{0:T(1024)S(1)} all-reduce(f32[4096]{0:T(1024)S(1)} %multiply_reduce_fusion.6), channel_id=1, replica_groups=mesh['dp'=8,'tensor'=4] {'tensor'}, use_global_device_ids=true, to_apply=%region_14.15 | all-reduce | flops 4096 | bytes 32768 | tf_op jit(solution)/shard_map/psum | solution.py:173
  422.8 5.6 multiply_reduce_fusion.2
  428.4 16.3 %all-reduce.3 = (bf16[4096]{0:T(1024)(128)(2,1)S(1)}, bf16[4096]{0:T(1024)(128)(2,1)S(1)}) all-reduce(bf16[4096]{0:T(1024)(128)(2,1)S(1)} %get-tuple-element.331, bf16[4096]{0:T(1024)(128)(2,1)S(1)} %get-tuple-element.335), channel_id=1, replica_groups=mesh['dp'=8,'tensor'=4] {'tensor'}, use_global_device_ids=true, to_apply=%region_18.19 | all-reduce | flops 8192 | bytes 32768 | tf_op jit(solution)/shard_map/psum | solution.py:182
  444.8 6.1 convert_reduce_fusion.1
  450.9 13.0 %convert_reduce_fusion = (f32[768]{0:T(1024)}, bf16[768,4096]{0,1:T(8,128)(2,1)S(1)}) fusion(f32[768,4096]{0,1:T(8,128)} %get-tuple-element.430, bf16[192,768]{1,0:T(8,128)(2,1)S(1)} %copy-done.52, f32[192,4096]{1,0:T(8,128)S(1)} %get-tuple-element.426, f32[4096,768]{1,0:T(8,128)} %get-tuple-element.446, f32[768]{0:T(1024)S(1)} %copy-done.53), kind=kOutput, calls=%fused_computation.75 | convolution fusion | flops 1262222592 | bytes 34904064 | tf_op jit(solution)/shard_map/dot_general | solution.py:24
  463.9 4.6 multiply_reduce_fusion.3
  468.5 15.6 %all-reduce.2 = (bf16[4096]{0:T(1024)(128)(2,1)S(1)}, bf16[4096]{0:T(1024)(128)(2,1)S(1)}) all-reduce(bf16[4096]{0:T(1024)(128)(2,1)S(1)} %get-tuple-element.333, bf16[4096]{0:T(1024)(128)(2,1)S(1)} %get-tuple-element.334), channel_id=1, replica_groups=mesh['dp'=8,'tensor'=4] {'tensor'}, use_global_device_ids=true, to_apply=%region_22.23 | all-reduce | flops 8192 | bytes 32768 | tf_op jit(solution)/shard_map/psum | solution.py:202
  484.1 4.9 convert_reduce_fusion.2
  489.3 6.0 fusion.63
  495.2 5.7 fusion.67
  501.0 102.2 %all-gather.2.cloned.1.call-done = bf16[768,4096]{1,0:T(8,128)(2,1)} async-done(((bf16[192,4096]{1,0:T(8,128)(2,1)}), bf16[768,4096]{1,0:T(8,128)(2,1)}) %all-gather.2.cloned.1.call-update) | async-done | bytes 6291472 | tf_op jit(solution)/shard_map/all_gather | solution.py:211
  603.1 4.2 fusion.61
  614.3 121.7 %while.60 = (s32[]{:T(128)}, bf16[4,3,64,1024]{3,2,1,0:T(8,128)(2,1)}, bf16[4,3,64,1024]{3,2,1,0:T(8,128)(2,1)}, bf16[4,3,64,1024]{3,2,1,0:T(8,128)(2,1)}, bf16[...) while((s32[]{:T(128)}, ...), condition=%wide.region_27.28_spmd, body=%wide.region_23.27_spmd.sunk | while | flops 1021868544 | bytes 70955544 | solution.py:219
  622.8 18.3 %while.62 = (s32[]{:T(128)}, f32[3,64,1024]{2,1,0:T(8,128)S(1)}, f32[3,64,1024]{2,1,0:T(8,128)S(1)}, bf16[2,3,64,512]{3,2,1,0:T(8,128)(2,1)}, bf16[2,3,64,512]{3...) while((s32[]{:T(128)}, f32[3,64,1024]{2,1,0:T(8,128)S(1)}, ...), condition=%wide.region_26.26_spmd.clone, body=%wide.region_24.25_spmd.clone.sunk | while | flops 1021868544 | bytes 59060492 | solution.py:102
  653.2 18.3 %while.62 = (s32[]{:T(128)}, f32[3,64,1024]{2,1,0:T(8,128)S(1)}, f32[3,64,1024]{2,1,0:T(8,128)S(1)}, bf16[2,3,64,512]{3,2,1,0:T(8,128)(2,1)}, bf16[2,3,64,512]{3...) while((s32[]{:T(128)}, f32[3,64,1024]{2,1,0:T(8,128)S(1)}, ...), condition=%wide.region_26.26_spmd.clone, body=%wide.region_24.25_spmd.clone.sunk | while | flops 1021868544 | bytes 59060492 | solution.py:102
  683.6 18.3 %while.62 = (s32[]{:T(128)}, f32[3,64,1024]{2,1,0:T(8,128)S(1)}, f32[3,64,1024]{2,1,0:T(8,128)S(1)}, bf16[2,3,64,512]{3,2,1,0:T(8,128)(2,1)}, bf16[2,3,64,512]{3...) while((s32[]{:T(128)}, f32[3,64,1024]{2,1,0:T(8,128)S(1)}, ...), condition=%wide.region_26.26_spmd.clone, body=%wide.region_24.25_spmd.clone.sunk | while | flops 1021868544 | bytes 59060492 | solution.py:102
  714.0 18.3 %while.62 = (s32[]{:T(128)}, f32[3,64,1024]{2,1,0:T(8,128)S(1)}, f32[3,64,1024]{2,1,0:T(8,128)S(1)}, bf16[2,3,64,512]{3,2,1,0:T(8,128)(2,1)}, bf16[2,3,64,512]{3...) while((s32[]{:T(128)}, f32[3,64,1024]{2,1,0:T(8,128)S(1)}, ...), condition=%wide.region_26.26_spmd.clone, body=%wide.region_24.25_spmd.clone.sunk | while | flops 1021868544 | bytes 59060492 | solution.py:102
  757.3 25.2 %all-reduce = (f32[192]{0:T(256)}, f32[192]{0:T(256)}, f32[192]{0:T(256)}, f32[192]{0:T(256)}, f32[192]{0:T(256)}, /*index=5*/f32[768]{0:T(1024)}, f32[192]{0:T(256)}, f32[192]{0:T(256)}, f32[192]{0:T(256)}) all-reduce(f32[192]{0:T(256)S(1)} %reduce_sum.184, f32[192]{0:T(256)S(1)} %reduce_sum.186, ...), channel_id=1, replica_groups=mesh['dp'=8,'tensor'=4] {'dp'}, use_global_device_ids=true, to_apply=%region_32.33 | all-reduce | flops 2304 | bytes 18432 | tf_op jit(solution)/shard_map/psum | solution.py:236
  789.5 30.4 %all-reduce.6.cloned.1.call-done = (f32[192,192]{1,0:T(8,128)}, f32[192,192]{1,0:T(8,128)}, f32[192,192]{1,0:T(8,128)}, f32[768,192]{0,1:T(8,128)}, f32[768,192]{0,1:T(8,128)}, /*index=5*/f32[192,768]{1,0:T(8,128)}) async-done(((f32[192,192]{1,0:T(8,128)}, f32[192,192]{1,0:T(8,128)}, f32[192,192]{1,0:T(8,128)}, f32[768,192]{0,1:T(8,128)}, f32[768,192]{0,1:T(8,128)}, /*index=5*/f32[192,768]{1,0:T(8,128)}), ...) | async-done | bytes 2211856 | tf_op jit(solution)/shard_map/psum | solution.py:236
  (477 shorter events, 243.8 us)
Async XLA Ops:
  7.2 345.8 %copy-start = (bf16[768,192]{0,1:T(8,128)(2,1)S(1)}, bf16[768,192]{0,1:T(8,128)(2,1)}, u32[]{:S(2)}) copy-start(bf16[768,192]{0,1:T(8,128)(2,1)} %param.36) | copy-start | bytes 884740
  7.2 308.3 %reduce-scatter.4.cloned.1.call-start = ((), (), s32[]{:S(2)}) async-start(), calls=%async_computation.2 | async-start | bytes 15728640 | tf_op jit(solution)/shard_map/reduce_scatter | solution.py:149
  10.4 4.6 copy-start.48
  100.7 214.8 %copy-start.49 = (f32[192]{0:T(256)S(1)}, f32[192]{0:T(256)}, u32[]{:S(2)}) copy-start(f32[192]{0:T(256)} %param.33) | copy-start | bytes 2308
  100.7 502.4 %all-gather.2.cloned.1.call-start = ((), (), s32[]{:S(2)}) async-start(), calls=%async_computation.1 | async-start | bytes 7864320 | tf_op jit(solution)/shard_map/all_gather | solution.py:211
  318.4 176.8 %copy-start.4 = (f32[192,4096]{1,0:T(8,128)}, f32[192,4096]{1,0:T(8,128)S(1)}, u32[]{:S(2)}) copy-start(f32[192,4096]{1,0:T(8,128)S(1)} %get-tuple-element.432) | copy-start | bytes 9437188
  318.4 34.6 %copy-start.38 = (f32[192]{0:T(256)S(1)}, f32[192]{0:T(256)}, u32[]{:S(2)}) copy-start(f32[192]{0:T(256)} %param.34) | copy-start | bytes 2308
  318.4 34.6 %copy-start.53 = (f32[768]{0:T(1024)S(1)}, f32[768]{0:T(1024)}, u32[]{:S(2)}) copy-start(f32[768]{0:T(1024)} %param.37) | copy-start | bytes 9220
  318.4 34.6 %copy-start.55 = (f32[192]{0:T(256)S(1)}, f32[192]{0:T(256)}, u32[]{:S(2)}) copy-start(f32[192]{0:T(256)} %param.35) | copy-start | bytes 2308
  337.1 158.1 %copy-start.22 = (f32[4096]{0:T(1024)}, f32[4096]{0:T(1024)S(1)}, u32[]{:S(2)}) copy-start(f32[4096]{0:T(1024)S(1)} %broadcast_multiply_fusion.1) | copy-start | bytes 49156
  353.0 142.2 %copy-start.25 = (f32[4096]{0:T(1024)}, f32[4096]{0:T(1024)S(1)}, u32[]{:S(2)}) copy-start(f32[4096]{0:T(1024)S(1)} %add_rsqrt_fusion.1) | copy-start | bytes 49156
  353.0 31.3 %copy-start.51 = (bf16[192,768]{1,0:T(8,128)(2,1)S(1)}, bf16[192,768]{1,0:T(8,128)(2,1)}, u32[]{:S(2)}) copy-start(bf16[192,768]{1,0:T(8,128)(2,1)} %param.38) | copy-start | bytes 884740
  353.0 31.3 %copy-start.54 = (f32[192]{0:T(256)S(1)}, f32[192]{0:T(256)}, u32[]{:S(2)}) copy-start(f32[192]{0:T(256)} %param.39) | copy-start | bytes 2308
  388.3 34.5 %copy-start.40 = (f32[192]{0:T(256)S(1)}, f32[192]{0:T(256)}, u32[]{:S(2)}) copy-start(f32[192]{0:T(256)} %param.40) | copy-start | bytes 2308
  422.8 22.0 %copy-start.50 = (f32[192]{0:T(256)S(1)}, f32[192]{0:T(256)}, u32[]{:S(2)}) copy-start(f32[192]{0:T(256)} %param.41) | copy-start | bytes 2308
  444.8 6.1 copy-start.52
  450.9 13.0 %copy-start.8 = (f32[192,4096]{1,0:T(8,128)}, f32[192,4096]{1,0:T(8,128)S(1)}, u32[]{:S(2)}) copy-start(f32[192,4096]{1,0:T(8,128)S(1)} %get-tuple-element.426) | copy-start | bytes 9437188
  484.0 4.9 copy-start.34
  484.1 4.9 copy-start.36
  489.0 330.9 %all-reduce.6.cloned.1.call-start = ((), (), s32[]{:S(2)}) async-start(), calls=%async_computation.3 | async-start | bytes 4718592 | tf_op jit(solution)/shard_map/psum | solution.py:236
  489.2 6.0 copy-start.56
  495.2 107.9 %copy-start.33 = (bf16[768,192]{0,1:T(8,128)(2,1)S(1)}, bf16[768,192]{0,1:T(8,128)(2,1)}, u32[]{:S(2)}) copy-start(bf16[768,192]{0,1:T(8,128)(2,1)} %param.32) | copy-start | bytes 884740
  746.7 7.3 slice-start
  754.1 28.4 %copy-start.5 = (f32[192,4096]{1,0:T(8,128)S(1)}, f32[192,4096]{1,0:T(8,128)}, u32[]{:S(2)}) copy-start(f32[192,4096]{1,0:T(8,128)} %copy-done.4) | copy-start | bytes 9437188
  754.1 28.4 %copy-start.23 = (f32[4096]{0:T(1024)S(1)}, f32[4096]{0:T(1024)}, u32[]{:S(2)}) copy-start(f32[4096]{0:T(1024)} %copy-done.22) | copy-start | bytes 49156
  754.1 28.4 %copy-start.26 = (f32[4096]{0:T(1024)S(1)}, f32[4096]{0:T(1024)}, u32[]{:S(2)}) copy-start(f32[4096]{0:T(1024)} %copy-done.25) | copy-start | bytes 49156
  754.2 28.4 %copy-start.27 = (bf16[192,192]{1,0:T(8,128)(2,1)S(1)}, bf16[192,192]{1,0:T(8,128)(2,1)}, u32[]{:S(2)}) copy-start(bf16[192,192]{1,0:T(8,128)(2,1)} %param.27) | copy-start | bytes 221188
  754.2 28.4 %copy-start.35 = (f32[4096]{0:T(1024)S(1)}, f32[4096]{0:T(1024)}, u32[]{:S(2)}) copy-start(f32[4096]{0:T(1024)} %copy-done.34) | copy-start | bytes 49156
  754.2 28.4 %copy-start.37 = (f32[4096]{0:T(1024)S(1)}, f32[4096]{0:T(1024)}, u32[]{:S(2)}) copy-start(f32[4096]{0:T(1024)} %copy-done.36) | copy-start | bytes 49156
  754.2 28.4 %copy-start.39 = (f32[192]{0:T(256)S(1)}, f32[192]{0:T(256)}, u32[]{:S(2)}) copy-start(f32[192]{0:T(256)} %param.34) | copy-start | bytes 2308
  787.7 41.7 %copy-start.1 = (bf16[768,192]{0,1:T(8,128)(2,1)S(1)}, bf16[768,192]{0,1:T(8,128)(2,1)}, u32[]{:S(2)}) copy-start(bf16[768,192]{0,1:T(8,128)(2,1)} %param.36) | copy-start | bytes 884740
  819.9 8.7 %copy-start.24 = (f32[192,768]{1,0:T(8,128)S(1)}, f32[192,768]{1,0:T(8,128)}, u32[]{:S(2)}) copy-start(f32[192,768]{1,0:T(8,128)} %get-tuple-element.879) | copy-start | bytes 1769476
  (58 other events, 124.6 us)
Sparse Core Ops, SparseCore 0:
  100.8 214.6 reduce-scatter.3
  489.1 113.9 all-gather.1
  757.4 62.4 all-reduce.5
where the time goes:
time: 845 us; the launch traced here: 836 us
  waiting for transfers between devices  347 us (41%)
  matrix products  184 us (22%)
  local copies, waits for them, and re-layouts  124 us (15%)
  blocking collectives  123 us (15%)
  other arithmetic  39.5 us (5%)
  between operations  15 us (2%)
    reduce_scatter x1, waiting for transfers between devices, shards(): lax.psum_scatter(jnp.dot(output_w, context_low, preferred_element_type=jn...  215 us
    all_gather x1, waiting for transfers between devices, shards(): piece = lax.all_gather(attended_grad_low, 'tensor', axis=0, tiled=True)  102 us
    dot_general x1, matrix products, shards(): jnp.dot(inner_w, hidden_low, preferred_element_type=jnp.float32)  31.2 us
    psum x1, waiting for transfers between devices, shards(): lax.psum((grad_query_w, grad_key_w, grad_value_w, grad_query_b, grad_valu...  30.4 us
    unnamed x121, local copies, waits for them, and re-layouts  30.3 us
    dot_general x16, matrix products, one_block(): jnp.einsum('hdq,hdk->hqk', query_part, keys, preferred_element_type=jnp.f...  30 us
    dot_general x6, matrix products, through_weight(): lax.dot_general(weight, grad, (((0,), (0,)), ((), ())), preferred_element...  27.8 us
    psum x1, blocking collectives, shards(): lax.psum((grad_query_w, grad_key_w, grad_value_w, grad_query_b, grad_valu...  25.2 us
  transfers between devices with their start and end apart: 3, of which 3 were waited for; matrix products, arithmetic and copies ran while one was open for 2% of the time, Pallas kernels for 0%

commit v1 on v0

v1 whole, which is shorter than its diff:
```python
from functools import partial

import jax
import jax.numpy as jnp
from jax import lax
from jax.experimental import pallas as pl
from jax.experimental.pallas import tpu as pltpu
from jax.sharding import PartitionSpec as P

D = 768
HDIM = 64
SEQ_LEN = 1024
EPSILON = 1e-05
SCALE = HDIM ** (-0.5)
CHUNK = 256
TOKEN_BLOCK = 256

F32 = jnp.float32
BF16 = jnp.bfloat16


def mm(left, right):
    return lax.dot_general(left, right, (((1,), (0,)), ((), ())), preferred_element_type=F32)


def mm_nt(left, right):
    return lax.dot_general(left, right, (((1,), (1,)), ((), ())), preferred_element_type=F32)


def mm_tn(left, right):
    return lax.dot_general(left, right, (((0,), (0,)), ((), ())), preferred_element_type=F32)


def attend_kernel(x_ref, w_ref, b_ref, qkv_ref, ctx_ref, expo_ref, inv_ref):
    rows = 3 * HDIM
    weight = w_ref[...].reshape(rows, w_ref.shape[2])
    bias = b_ref[...].reshape(rows, 1)
    low = (mm(weight, x_ref[...]) + bias).astype(BF16)
    qkv_ref[...] = low.reshape(3, HDIM, low.shape[1])
    query = low[:HDIM] * BF16(SCALE)
    keys = low[HDIM : 2 * HDIM]
    values = low[2 * HDIM :]
    for start in range(0, low.shape[1], CHUNK):
        part = slice(start, start + CHUNK)
        scores = mm_tn(keys, query[:, part])
        expo = jnp.exp(scores - jnp.max(scores, axis=0, keepdims=True))
        inv = 1.0 / jnp.sum(expo, axis=0, keepdims=True)
        expo_low = expo.astype(BF16)
        expo_ref[0, :, part] = expo_low
        inv_ref[0, :, part] = inv
        ctx_ref[:, part] = (mm(values, expo_low) * inv).astype(BF16)


def attend(x, weight, bias):
    local, length = x.shape
    heads = local // HDIM
    return pl.pallas_call(
        attend_kernel,
        grid=(heads,),
        in_specs=[
            pl.BlockSpec((local, length), lambda h: (0, 0)),
            pl.BlockSpec((3, HDIM, local), lambda h: (0, h, 0)),
            pl.BlockSpec((3, HDIM, 1), lambda h: (0, h, 0)),
        ],
        out_specs=[
            pl.BlockSpec((3, HDIM, length), lambda h: (0, h, 0)),
            pl.BlockSpec((HDIM, length), lambda h: (h, 0)),
            pl.BlockSpec((1, length, length), lambda h: (h, 0, 0)),
            pl.BlockSpec((1, 1, length), lambda h: (h, 0, 0)),
        ],
        out_shape=[
            jax.ShapeDtypeStruct((3, local, length), BF16),
            jax.ShapeDtypeStruct((local, length), BF16),
            jax.ShapeDtypeStruct((heads, length, length), BF16),
            jax.ShapeDtypeStruct((heads, 1, length), F32),
        ],
        name="attend",
    )(x, weight, bias)


def attend_back_kernel(
    x_ref, w_ref, qkv_ref, ctx_ref, expo_ref, inv_ref, grad_ref, resid_ref, out_ref, gw_ref, gb_ref, acc_ref
):
    head = pl.program_id(0)
    rows = 3 * HDIM
    length = x_ref.shape[1]
    query = qkv_ref[0]
    keys = qkv_ref[1]
    values = qkv_ref[2]
    scaled = (grad_ref[...].astype(F32) * inv_ref[0]).astype(BF16)
    delta = jnp.sum(scaled.astype(F32) * ctx_ref[...].astype(F32), axis=0, keepdims=True)
    grad_keys = jnp.zeros((HDIM, length), F32)
    grad_values = jnp.zeros((HDIM, length), F32)
    grad_query = []
    for start in range(0, length, CHUNK):
        part = slice(start, start + CHUNK)
        expo = expo_ref[0, :, part]
        grad_probs = mm_tn(values, scaled[:, part])
        grad_scores = (expo.astype(F32) * (grad_probs - delta[:, part])).astype(BF16)
        grad_query.append((mm(keys, grad_scores) * SCALE).astype(BF16))
        grad_keys += mm_nt(query[:, part], grad_scores)
        grad_values += mm_nt(scaled[:, part], expo)
    low = jnp.concatenate(
        [
            jnp.concatenate(grad_query, axis=1),
            (grad_keys * SCALE).astype(BF16),
            grad_values.astype(BF16),
        ],
        axis=0,
    )
    gw_ref[...] = mm_nt(low, x_ref[...]).reshape(3, HDIM, x_ref.shape[0])
    gb_ref[...] = jnp.sum(low.astype(F32), axis=1, keepdims=True).reshape(3, HDIM, 1)
    step = mm_tn(w_ref[...].reshape(rows, x_ref.shape[0]), low)

    @pl.when(head == 0)
    def _():
        acc_ref[...] = resid_ref[...] + step

    @pl.when(head > 0)
    def _():
        acc_ref[...] += step

    @pl.when(head == pl.num_programs(0) - 1)
    def _():
        out_ref[...] = acc_ref[...].astype(BF16)


def attend_back(x, weight, qkv, context, expo, inv, grad_context, grad_resid):
    local, length = x.shape
    heads = local // HDIM
    return pl.pallas_call(
        attend_back_kernel,
        grid=(heads,),
        in_specs=[
            pl.BlockSpec((local, length), lambda h: (0, 0)),
            pl.BlockSpec((3, HDIM, local), lambda h: (0, h, 0)),
            pl.BlockSpec((3, HDIM, length), lambda h: (0, h, 0)),
            pl.BlockSpec((HDIM, length), lambda h: (h, 0)),
            pl.BlockSpec((1, length, length), lambda h: (h, 0, 0)),
            pl.BlockSpec((1, 1, length), lambda h: (h, 0, 0)),
            pl.BlockSpec((HDIM, length), lambda h: (h, 0)),
            pl.BlockSpec((local, length), lambda h: (0, 0)),
        ],
        out_specs=[
            pl.BlockSpec((local, length), lambda h: (0, 0)),
            pl.BlockSpec((3, HDIM, local), lambda h: (0, h, 0)),
            pl.BlockSpec((3, HDIM, 1), lambda h: (0, h, 0)),
        ],
        out_shape=[
            jax.ShapeDtypeStruct((local, length), BF16),
            jax.ShapeDtypeStruct((3, local, local), F32),
            jax.ShapeDtypeStruct((3, local, 1), F32),
        ],
        scratch_shapes=[pltpu.VMEM((local, length), F32)],
        name="attend_back",
    )(x, weight, qkv, context, expo, inv, grad_context, grad_resid)


def normal_parts(v):
    expo = jnp.exp(-0.5 * v * v)
    t = 1.0 / (1.0 + (0.3275911 * 0.5**0.5) * jnp.abs(v))
    poly = t * (
        0.127414796 + t * (-0.142248368 + t * (0.7107068705 + t * (-0.7265760135 + t * 0.5307027145)))
    )
    tail = poly * expo
    return jnp.where(v >= 0, 1.0 - tail, tail), expo * 0.3989422804014327


V_OUT_B, V_GAIN1, V_SHIFT1, V_OUTER_B, V_GAIN2, V_SHIFT2, V_INNER_B = range(7)
G_OUT_B, G_GAIN1, G_SHIFT1, G_OUTER_B, G_GAIN2, G_INNER_B = range(6)


def middle_kernel(
    groups,
    rank_ref,
    *refs,
):
    x_refs = refs[:groups]
    ctx_refs = refs[groups : 2 * groups]
    cot_refs = refs[2 * groups : 3 * groups]
    w_ref, vec_ref = refs[3 * groups : 3 * groups + 2]
    refs = refs[3 * groups + 2 :]
    out_refs = refs[:groups]
    grad_refs = refs[groups : 2 * groups]
    resid_refs = refs[2 * groups : 3 * groups]
    gw_ref, gv_ref, act_ref, dact_ref = refs[3 * groups :]
    span = range(groups)
    local = x_refs[0].shape[0]
    hidden = w_ref.shape[2]
    first = pl.program_id(0) == 0
    rank = rank_ref[0]
    rows = [pl.ds(pl.multiple_of(lax.rem(rank + r, groups) * local, local), local) for r in span]

    @pl.when(first)
    def _():
        gw_ref[...] = jnp.zeros_like(gw_ref)
        gv_ref[...] = jnp.zeros_like(gv_ref)

    def vec(r, which):
        return vec_ref[r, :, which : which + 1]

    def total(parts):
        return sum(jnp.sum(p, axis=0, keepdims=True) for p in parts)

    def add_vec(r, which, array):
        gv_ref[r, :, which : which + 1] += jnp.sum(array, axis=1, keepdims=True)

    ctx = [ctx_refs[r][...] for r in span]
    resid = []
    for o in span:
        attended = sum(mm(w_ref[r, 0, rows[o], :], ctx[r]) for r in span)
        resid.append(x_refs[o][...].astype(F32) + attended + vec(o, V_OUT_B))
    center = total(resid) / D
    offset = [p - center for p in resid]
    inv1 = lax.rsqrt(total([p * p for p in offset]) / D + EPSILON)
    normed1 = [p * inv1 for p in offset]
    low1 = []
    resid2 = []
    for r in span:
        hid = normed1[r] * vec(r, V_GAIN1) + vec(r, V_SHIFT1)
        low = hid.astype(BF16)
        low1.append(low)
        inner = mm(w_ref[r, 1], low)
        outer = hid + vec(r, V_OUTER_B)
        for part in range(hidden // local):
            at = slice(part * local, (part + 1) * local)
            v = inner[at] + vec(r, V_INNER_B + part)
            cdf, density = normal_parts(v)
            act = (v * cdf).astype(BF16)
            act_ref[r, at, :] = act
            dact_ref[r, at, :] = cdf + v * density
        outer += mm_tn(w_ref[r, 2], act_ref[r])
        resid2.append(outer)
    center = total(resid2) / D
    offset = [p - center for p in resid2]
    inv2 = lax.rsqrt(total([p * p for p in offset]) / D + EPSILON)
    normed2 = [p * inv2 for p in offset]
    scaled = []
    for r in span:
        out_refs[r][...] = (normed2[r] * vec(r, V_GAIN2) + vec(r, V_SHIFT2)).astype(BF16)
        cot = cot_refs[r][...].astype(F32)
        add_vec(r, G_GAIN2, cot * normed2[r])
        scaled.append(cot * vec(r, V_GAIN2))
    mean = total(scaled) / D
    slope = total([scaled[r] * normed2[r] for r in span]) / D
    grad1 = []
    for r in span:
        grad2 = inv2 * (scaled[r] - mean - normed2[r] * slope)
        grad2_low = grad2.astype(BF16)
        add_vec(r, G_OUTER_B, grad2_low.astype(F32))
        gw_ref[r, 2] += mm_nt(act_ref[r], grad2_low)
        grad_act = mm(w_ref[r, 2], grad2_low)
        pieces = []
        for part in range(hidden // local):
            at = slice(part * local, (part + 1) * local)
            piece = (grad_act[at] * dact_ref[r, at, :]).astype(BF16)
            add_vec(r, G_INNER_B + part, piece.astype(F32))
            pieces.append(piece)
        inner_low = jnp.concatenate(pieces, axis=0)
        gw_ref[r, 1] += mm_nt(inner_low, low1[r])
        grad = grad2 + mm_tn(w_ref[r, 1], inner_low)
        add_vec(r, G_GAIN1, grad * normed1[r])
        add_vec(r, G_SHIFT1, grad)
        grad1.append(grad)
    scaled = [grad1[r] * vec(r, V_GAIN1) for r in span]
    mean = total(scaled) / D
    slope = total([scaled[r] * normed1[r] for r in span]) / D
    lows = []
    for r in span:
        grad = inv1 * (scaled[r] - mean - normed1[r] * slope)
        resid_refs[r][...] = grad
        low = grad.astype(BF16)
        lows.append(low)
        add_vec(r, G_OUT_B, low.astype(F32))
    for r in span:
        context_grad = sum(mm_tn(w_ref[r, 0, rows[o], :], lows[o]) for o in span)
        grad_refs[r][...] = context_grad.astype(BF16)
        for o in span:
            gw_ref[r, 0, rows[o], :] += mm_nt(lows[o], ctx[r])


def middle(rank, xs, contexts, cots, weights, vecs):
    groups = len(xs)
    local, length = xs[0].shape
    hidden = weights.shape[2]
    block = pl.BlockSpec((local, TOKEN_BLOCK), lambda t, rank: (0, t))
    whole = lambda shape: pl.BlockSpec(
        shape, lambda t, rank: (0,) * len(shape), pipeline_mode=pl.Buffered(1)
    )
    grad_vecs = (groups, local, G_INNER_B + hidden // local)
    piece = lambda dtype: jax.ShapeDtypeStruct((local, length), dtype)
    outs = pl.pallas_call(
        partial(middle_kernel, groups),
        grid_spec=pltpu.PrefetchScalarGridSpec(
            num_scalar_prefetch=1,
            grid=(length // TOKEN_BLOCK,),
            in_specs=[block] * (3 * groups) + [whole(weights.shape), whole(vecs.shape)],
            out_specs=[block] * (3 * groups) + [whole(weights.shape), whole(grad_vecs)],
            scratch_shapes=[
                pltpu.VMEM((groups, hidden, TOKEN_BLOCK), BF16),
                pltpu.VMEM((groups, hidden, TOKEN_BLOCK), F32),
            ],
        ),
        out_shape=[piece(BF16)] * (2 * groups)
        + [piece(F32)] * groups
        + [
            jax.ShapeDtypeStruct(weights.shape, F32),
            jax.ShapeDtypeStruct(grad_vecs, F32),
        ],
        name="middle",
    )(rank, *xs, *contexts, *cots, weights, vecs)
    return (
        outs[:groups],
        outs[groups : 2 * groups],
        outs[2 * groups : 3 * groups],
        outs[3 * groups],
        outs[3 * groups + 1],
    )


def shards(
    inputs,
    cotangent,
    query_w,
    key_w,
    value_w,
    query_b,
    value_b,
    output_w,
    output_b,
    first_gain,
    first_shift,
    inner_w,
    inner_b,
    outer_w,
    outer_b,
    second_gain,
    second_shift,
):
    groups = lax.axis_size("tensor")
    rank = lax.axis_index("tensor")
    number = lax.axis_size("dp")
    place = lax.axis_index("dp")
    local, tokens = inputs.shape
    length = tokens // groups
    span = range(groups)
    assert length == SEQ_LEN

    def from_group(piece, r):
        if r == 0:
            return piece
        return lax.ppermute(piece, "tensor", [(i, (i - r) % groups) for i in span])

    def to_group(piece, r):
        if r == 0:
            return piece
        return lax.ppermute(piece, "tensor", [(i, (i + r) % groups) for i in span])

    def swap(piece, bit):
        return lax.ppermute(piece, "dp", [(i, i ^ bit) for i in range(number)])

    def part_for(array, r):
        owner = lax.rem(rank + groups - r, groups)
        return lax.dynamic_slice_in_dim(array, owner * length, length, 1)

    def assemble(pieces):
        whole = jnp.zeros((local, tokens), pieces[0].dtype)
        for r in span:
            owner = lax.rem(rank + groups - r, groups)
            whole = lax.dynamic_update_slice_in_dim(whole, to_group(pieces[r], r), owner * length, 1)
        return whole

    def half(array, bit, other):
        size = array.shape[1] // 2
        which = lax.rem(lax.div(place, bit), 2)
        which = 1 - which if other else which
        return lax.dynamic_slice_in_dim(array, which * size, size, 1)

    def join(mine, got, bit, axis):
        first = lax.rem(lax.div(place, bit), 2) == 0
        return jnp.where(
            first,
            jnp.concatenate([mine, got], axis=axis),
            jnp.concatenate([got, mine], axis=axis),
        )

    bits = [1 << k for k in range(number.bit_length() - 1)]
    mirrored = sum(lax.rem(lax.div(place, bit), 2) * (number // 2 // bit) for bit in bits)

    def all_groups(shard, axis):
        size = shard.shape[axis] // number
        mine = lax.dynamic_slice_in_dim(shard, mirrored * size, size, axis)
        held = jnp.stack([from_group(mine, r) for r in span[1:]])
        for bit in reversed(bits):
            held = join(held, swap(held, bit), bit, axis + 1)
        return [shard] + [held[r - 1] for r in span[1:]]

    def reduce_groups(parts):
        for bit in bits:
            got = swap(half(parts, bit, True).astype(BF16), bit)
            parts = half(parts, bit, False) + got.astype(F32)
        total = parts[0]
        for r in span[1:]:
            total = total + to_group(parts[r].astype(BF16), r).astype(F32)
        for bit in reversed(bits):
            total = join(total, swap(total, bit), bit, 0)
        return total

    xs = [from_group(part_for(inputs, r), r) for r in span]
    vec_shard = jnp.concatenate(
        [
            jnp.stack(
                [
                    output_b,
                    first_gain,
                    first_shift,
                    outer_b,
                    second_gain,
                    second_shift,
                ]
            ),
            inner_b.reshape(-1, local),
            jnp.stack([query_b, jnp.zeros_like(query_b), value_b]),
        ]
    )
    vec_rows = [from_group(vec_shard, r) for r in span]
    qkv_w = all_groups(jnp.stack([query_w, key_w, value_w]), 1)
    mid_w = all_groups(jnp.stack([output_w, inner_w, outer_w.T]), 1)
    cot_low = cotangent.astype(BF16)
    cots = [from_group(part_for(cot_low, r), r) for r in span]

    saved = []
    for r in span:
        bias = vec_rows[r][-3:][:, :, None]
        saved.append(attend(xs[r], qkv_w[r], bias))
    vecs = jnp.swapaxes(jnp.stack([rows[:-3] for rows in vec_rows]), 1, 2)
    outs, grad_contexts, grad_resids, grad_mid_w, grad_vecs = middle(
        rank.reshape(1), xs, [s[1] for s in saved], cots, jnp.stack(mid_w), vecs
    )
    layer_out = assemble(outs)
    backs = [None] * groups
    for r in (2, 3, 1, 0):
        qkv, context, expo, inv = saved[r]
        backs[r] = attend_back(
            xs[r], qkv_w[r], qkv, context, expo, inv, grad_contexts[r], grad_resids[r]
        )
    input_grad = assemble([b[0] for b in backs])

    mid = reduce_groups(grad_mid_w.reshape(groups, -1, local)).reshape(3, -1, local)
    qkv = reduce_groups(jnp.stack([b[1].reshape(-1, local) for b in backs])).reshape(3, local, local)
    rows = jnp.concatenate(
        [
            jnp.swapaxes(grad_vecs, 1, 2),
            jnp.stack([b[2][:, :, 0] for b in backs]),
        ],
        axis=1,
    )
    count = rows.shape[1]
    mine = sum(to_group(rows[r], r) for r in span)
    shift = jnp.sum(cotangent, axis=1)
    small = lax.psum(jnp.concatenate([mine, shift[None]]), "dp")
    hidden = inner_b.shape[0] // local
    inner_rows = small[G_INNER_B : G_INNER_B + hidden].reshape(-1)
    return (
        layer_out,
        input_grad,
        qkv[0],
        qkv[1],
        qkv[2],
        small[count - 3],
        small[count - 1],
        mid[0],
        small[G_OUT_B],
        small[G_GAIN1],
        small[G_SHIFT1],
        mid[1],
        inner_rows,
        mid[2].T,
        small[G_OUTER_B],
        small[G_GAIN2],
        small[count],
    )


def solution(mesh):
    wide = P("tensor", "dp")
    rows = P("tensor", None)
    flat = P("tensor")
    columns = P(None, "tensor")
    return jax.shard_map(
        shards,
        mesh=mesh,
        in_specs=(
            wide,
            wide,
            rows,
            rows,
            rows,
            flat,
            flat,
            columns,
            flat,
            flat,
            flat,
            rows,
            flat,
            rows,
            flat,
            flat,
            flat,
        ),
        out_specs=(
            wide,
            wide,
            rows,
            rows,
            rows,
            flat,
            flat,
            columns,
            flat,
            flat,
            flat,
            rows,
            flat,
            rows,
            flat,
            flat,
            flat,
        ),
        check_vma=False,
    )
```

time: 845 us -> 407 us (0.48)
  the two profiles are of different devices: /device:TPU:0 before, /device:TPU:11 now
where the time goes in v1:
time: 407 us; the launch traced here: 399 us
  Pallas kernels  141 us (35%)
  waiting for transfers between devices  67.5 us (17%)
  local copies, waits for them, and re-layouts  60.8 us (15%)
  starting transfers between devices  59.5 us (15%)
  blocking collectives  40.7 us (10%)
  other arithmetic  27.6 us (7%)
    pallas_call x4, Pallas kernels, attend_back(): pl.pallas_call(attend_back_kernel, grid=(heads,), in_specs=[pl.BlockSpec(...  50.8 us
    pallas_call x4, Pallas kernels, attend(): pl.pallas_call(attend_kernel, grid=(heads,), in_specs=[pl.BlockSpec((loca...  49.6 us
    ppermute x18, waiting for transfers between devices, swap(): return lax.ppermute(piece, 'dp', [(i, i ^ bit) for i in range(number)])  45.9 us
    psum x1, blocking collectives, shards(): small = lax.psum(jnp.concatenate([mine, shift[None]]), 'dp')  40.7 us
    pallas_call x1, Pallas kernels, middle(): pl.pallas_call(partial(middle_kernel, groups), grid_spec=pltpu.PrefetchSc...  40.5 us
    ppermute x18, starting transfers between devices, swap(): return lax.ppermute(piece, 'dp', [(i, i ^ bit) for i in range(number)])  26.7 us
    ppermute x15, waiting for transfers between devices, to_group(): return lax.ppermute(piece, 'tensor', [(i, (i + r) % groups) for i in span])  20.8 us
    ppermute x15, starting transfers between devices, from_group(): return lax.ppermute(piece, 'tensor', [(i, (i - r) % groups) for i in span])  17.6 us
  transfers between devices with their start and end apart: 48, of which 15 were waited for; matrix products, arithmetic and copies ran while one was open for 18% of the time, Pallas kernels for 25%

profile of v1, /device:TPU:11, one launch (start us, length us, event | category | flops | bytes accessed | tf_op | source)
XLA Modules:
  0.0 398.9 jit_solution(387721734683456336)
XLA Ops:
  17.7 12.4 %attend.4 = (bf16[3,192,1024]{2,1,0:T(8,128)(2,1)}, bf16[192,1024]{1,0:T(8,128)(2,1)}, bf16[3,1024,1024]{2,1,0:T(8,128)(2,1)}, f32[3,1,1024]{2,1,0:T(1,128)}) custom-call(bf16[192,1024]{1,0:T(8,128)(2,1)} %get-tuple-element.116.x_ref.refs_0_, bf16[3,192,192]{2,1,0:T(8,128)(2,1)} %copy-done.10, f32[3,192,1]{2,1,0:T(8,128)} %copy.115.b_ref), custom_call_target="tpu_custom_call" | custom-call | tf_op jit(solution)/shard_map/attend/pallas_call | solution.py:57
  36.9 6.3 %collective-permute-done.18 = bf16[3,3,96,192]{3,2,1,0:T(8,128)(2,1)S(1)} collective-permute-done((bf16[3,3,96,192]{3,2,1,0:T(8,128)(2,1)S(1)}, bf16[3,3,96,192]{3,2,1,0:T(8,128)(2,1)S(1)}, u32[]{:S(2)}, u32[]{:S(2)}) %collective-permute-start.18) | collective-permute-done | bytes 331808 | tf_op jit(solution)/shard_map/ppermute | solution.py:360
  48.3 3.0 collective-permute-start.10
  54.7 9.1 %collective-permute-done.19 = bf16[3,3,192,192]{3,2,1,0:T(8,128)(2,1)S(1)} collective-permute-done((bf16[3,3,192,192]{3,2,1,0:T(8,128)(2,1)S(1)}, bf16[3,3,192,192]{3,2,1,0:T(8,128)(2,1)S(1)}, u32[]{:S(2)}, u32[]{:S(2)}) %collective-permute-start.19) | collective-permute-done | bytes 663584 | tf_op jit(solution)/shard_map/ppermute | solution.py:360
  66.4 4.9 %collective-permute-start.20 = (bf16[3,3,384,192]{2,3,1,0:T(8,128)(2,1)}, bf16[3,3,384,192]{2,3,1,0:T(8,128)(2,1)}, u32[]{:S(2)}, u32[]{:S(2)}) collective-permute-start(bf16[3,3,384,192]{2,3,1,0:T(8,128)(2,1)} %copy.128), channel_id=1, source_target_pairs={{0,4},{4,0},{8,12},{12,8},{16,20},{20,16},{24,28},{28,24},{1,5},{5... | collective-permute-start | bytes 3981320 | tf_op jit(solution)/shard_map/ppermute | solution.py:360
  75.3 5.7 %collective-permute-done.7 = bf16[3,3,48,192]{3,2,1,0:T(8,128)(2,1)S(1)} collective-permute-done((bf16[3,3,48,192]{3,2,1,0:T(8,128)(2,1)S(1)}, bf16[3,3,48,192]{3,2,1,0:T(8,128)(2,1)S(1)}, u32[]{:S(2)}, u32[]{:S(2)}) %collective-permute-start.7) | collective-permute-done | bytes 165920 | tf_op jit(solution)/shard_map/ppermute | solution.py:360
  84.1 2.9 copy.121.b_ref
  87.0 2.9 copy.124.b_ref
  90.0 2.9 copy.118.b_ref
  92.9 3.3 collective-permute-start.12
  99.4 12.4 %attend.6 = (bf16[3,192,1024]{2,1,0:T(8,128)(2,1)}, bf16[192,1024]{1,0:T(8,128)(2,1)}, bf16[3,1024,1024]{2,1,0:T(8,128)(2,1)}, f32[3,1,1024]{2,1,0:T(1,128)}) custom-call(bf16[192,1024]{1,0:T(8,128)(2,1)} %copy-done.5, bf16[3,192,192]{2,1,0:T(8,128)(2,1)} %get-tuple-element.121.w_ref, f32[3,192,1]{2,1,0:T(8,128)} %copy.121.b_ref), custom_call_target="tpu_custom_call" | custom-call | tf_op jit(solution)/shard_map/attend/pallas_call | solution.py:57
  112.6 12.4 %attend.7 = (bf16[3,192,1024]{2,1,0:T(8,128)(2,1)}, bf16[192,1024]{1,0:T(8,128)(2,1)}, bf16[3,1024,1024]{2,1,0:T(8,128)(2,1)}, f32[3,1,1024]{2,1,0:T(1,128)}) custom-call(bf16[192,1024]{1,0:T(8,128)(2,1)} %copy-done.7, bf16[3,192,192]{2,1,0:T(8,128)(2,1)} %get-tuple-element.120.w_ref, f32[3,192,1]{2,1,0:T(8,128)} %copy.124.b_ref), custom_call_target="tpu_custom_call" | custom-call | tf_op jit(solution)/shard_map/attend/pallas_call | solution.py:57
  125.7 12.4 %attend.5 = (bf16[3,192,1024]{2,1,0:T(8,128)(2,1)}, bf16[192,1024]{1,0:T(8,128)(2,1)}, bf16[3,1024,1024]{2,1,0:T(8,128)(2,1)}, f32[3,1,1024]{2,1,0:T(1,128)}) custom-call(bf16[192,1024]{1,0:T(8,128)(2,1)} %copy-done.6, bf16[3,192,192]{2,1,0:T(8,128)(2,1)} %get-tuple-element.122.w_ref, f32[3,192,1]{2,1,0:T(8,128)} %copy.118.b_ref), custom_call_target="tpu_custom_call" | custom-call | tf_op jit(solution)/shard_map/attend/pallas_call | solution.py:57
  145.1 40.5 %middle.1 = (bf16[192,1024]{1,0:T(8,128)(2,1)}, bf16[192,1024]{1,0:T(8,128)(2,1)}, bf16[192,1024]{1,0:T(8,128)(2,1)}, bf16[192,1024]{1,0:T(8,128)(2,1)}, bf16[19...) custom-call(s32[1]{0:T(128)} %bitcast.rank_ref, ...), custom_call_target="tpu_custom_call" | custom-call | tf_op jit(solution)/shard_map/middle/pallas_call | solution.py:292
  191.3 4.8 %constant_dynamic-slice_fusion.1 = f32[4,1152,192]{2,1,0:T(8,128)} fusion(f32[4,2304,192]{2,1,0:T(8,128)} %bitcast.108, s32[]{:T(128)S(6)} %select_n.191), kind=kLoop, calls=%fused_computation.74 | loop fusion | bytes 7077892 | tf_op jit(solution)/shard_map/dynamic_slice | solution.py:377
  196.1 3.8 copy.142
  199.9 12.9 %attend_back.7 = (bf16[192,1024]{1,0:T(8,128)(2,1)}, f32[3,192,192]{2,1,0:T(8,128)}, f32[3,192,1]{2,1,0:T(8,128)}) custom-call(bf16[192,1024]{1,0:T(8,128)(2,1)} %copy-done.7, bf16[3,192,192]{2,1,0:T(8,128)(2,1)} %get-tuple-element.120.w_ref, bf16[3,192,1024]{2,1,0:T(8,128)(2,1)} %get-tuple-element.85.qkv_ref, ...), custom_call_target="tpu_custom_call" | custom-call | tf_op jit(solution)/shard_map/attend_back/pallas_call | solution.py:131
  213.9 12.7 %attend_back.6 = (bf16[192,1024]{1,0:T(8,128)(2,1)}, f32[3,192,192]{2,1,0:T(8,128)}, f32[3,192,1]{2,1,0:T(8,128)}) custom-call(bf16[192,1024]{1,0:T(8,128)(2,1)} %copy-done.5, bf16[3,192,192]{2,1,0:T(8,128)(2,1)} %get-tuple-element.121.w_ref, bf16[3,192,1024]{2,1,0:T(8,128)(2,1)} %get-tuple-element.79.qkv_ref, ...), custom_call_target="tpu_custom_call" | custom-call | tf_op jit(solution)/shard_map/attend_back/pallas_call | solution.py:131
  228.3 12.6 %attend_back.5 = (bf16[192,1024]{1,0:T(8,128)(2,1)}, f32[3,192,192]{2,1,0:T(8,128)}, f32[3,192,1]{2,1,0:T(8,128)}) custom-call(bf16[192,1024]{1,0:T(8,128)(2,1)} %copy-done.6, bf16[3,192,192]{2,1,0:T(8,128)(2,1)} %get-tuple-element.122.w_ref, bf16[3,192,1024]{2,1,0:T(8,128)(2,1)} %get-tuple-element.73.qkv_ref, ...), custom_call_target="tpu_custom_call" | custom-call | tf_op jit(solution)/shard_map/attend_back/pallas_call | solution.py:131
  242.7 12.6 %attend_back.4 = (bf16[192,1024]{1,0:T(8,128)(2,1)}, f32[3,192,192]{2,1,0:T(8,128)}, f32[3,192,1]{2,1,0:T(8,128)}) custom-call(bf16[192,1024]{1,0:T(8,128)(2,1)} %get-tuple-element.116.x_ref.refs_0_, bf16[3,192,192]{2,1,0:T(8,128)(2,1)} %copy-done.10, bf16[3,192,1024]{2,1,0:T(8,128)(2,1)} %get-tuple-element.67.qkv_ref, ...), custom_call_target="tpu_custom_call" | custom-call | tf_op jit(solution)/shard_map/attend_back/pallas_call | solution.py:131
  277.6 40.7 %psum.7 = f32[13,192]{1,0:T(8,128)S(1)} all-reduce(f32[13,192]{1,0:T(8,128)S(1)} %pad_maximum_fusion.7), channel_id=1, replica_groups=mesh['dp'=8,'tensor'=4] {'dp'}, use_global_device_ids=true, to_apply=%region_1.2 | all-reduce | flops 2496 | bytes 19968 | tf_op jit(solution)/shard_map/psum | solution.py:461
  325.9 4.3 %collective-permute-done.28 = bf16[4,144,192]{2,1,0:T(8,128)(2,1)S(1)} collective-permute-done((bf16[4,144,192]{2,1,0:T(8,128)(2,1)S(1)}, bf16[4,144,192]{2,1,0:T(8,128)(2,1)S(1)}, u32[]{:S(2)}, u32[]{:S(2)}) %collective-permute-start.28) | collective-permute-done | bytes 221216 | tf_op jit(solution)/shard_map/ppermute | solution.py:360
  330.2 5.2 %collective-permute-done.41 = bf16[4,288,192]{1,2,0:T(8,128)(2,1)S(1)} collective-permute-done((bf16[4,288,192]{1,2,0:T(8,128)(2,1)S(1)}, bf16[4,288,192]{1,2,0:T(8,128)(2,1)S(1)}, u32[]{:S(2)}, u32[]{:S(2)}) %collective-permute-start.41) | collective-permute-done | bytes 442400 | tf_op jit(solution)/shard_map/ppermute | solution.py:360
  340.0 7.9 %collective-permute-done.43 = bf16[288,192]{0,1:T(8,128)(2,1)S(1)} collective-permute-done((bf16[288,192]{0,1:T(8,128)(2,1)S(1)}, bf16[288,192]{0,1:T(8,128)(2,1)S(1)}, u32[]{:S(2)}, u32[]{:S(2)}) %collective-permute-start.43) | collective-permute-done | bytes 110624 | tf_op jit(solution)/shard_map/ppermute | solution.py:357
  347.8 3.3 collective-permute-done.44
  351.4 6.9 %collective-permute-done.45 = f32[288,192]{0,1:T(8,128)S(1)} collective-permute-done((f32[288,192]{0,1:T(8,128)S(1)}, f32[288,192]{0,1:T(8,128)S(1)}, u32[]{:S(2)}, u32[]{:S(2)}) %collective-permute-start.45) | collective-permute-done | bytes 221216 | tf_op jit(solution)/shard_map/ppermute | solution.py:360
  358.5 5.1 %collective-permute-start.46 = (f32[576,192]{0,1:T(8,128)S(1)}, f32[576,192]{0,1:T(8,128)S(1)}, u32[]{:S(2)}, u32[]{:S(2)}) collective-permute-start(f32[576,192]{0,1:T(8,128)S(1)} %maximum_select_fusion.7), channel_id=1, source_target_pairs={{0,8},{4,12},{8,0},{12,4},{16,24},{20,28},{24,16},{28,20},{1,9},{5... | collective-permute-start | bytes 1327112 | tf_op jit(solution)/shard_map/ppermute | solution.py:360
  369.4 4.4 %collective-permute-done.46 = f32[576,192]{0,1:T(8,128)S(1)} collective-permute-done((f32[576,192]{0,1:T(8,128)S(1)}, f32[576,192]{0,1:T(8,128)S(1)}, u32[]{:S(2)}, u32[]{:S(2)}) %collective-permute-start.46) | collective-permute-done | bytes 442400 | tf_op jit(solution)/shard_map/ppermute | solution.py:360
  374.2 5.2 %collective-permute-start.47 = (f32[1152,192]{0,1:T(8,128)S(1)}, f32[1152,192]{0,1:T(8,128)S(1)}, u32[]{:S(2)}, u32[]{:S(2)}) collective-permute-start(f32[1152,192]{0,1:T(8,128)S(1)} %maximum_select_fusion.5), channel_id=1, source_target_pairs={{0,4},{4,0},{8,12},{12,8},{16,20},{20,16},{24,28},{28,24},{1,5},{5... | collective-permute-start | bytes 2654216 | tf_op jit(solution)/shard_map/ppermute | solution.py:360
  379.5 3.9 collective-permute-done.34
  383.5 4.4 %collective-permute-start.35 = (f32[288,192]{1,0:T(8,128)S(1)}, f32[288,192]{1,0:T(8,128)S(1)}, u32[]{:S(2)}, u32[]{:S(2)}) collective-permute-start(f32[288,192]{1,0:T(8,128)S(1)} %maximum_select_fusion.9), channel_id=1, source_target_pairs={{0,4},{4,0},{8,12},{12,8},{16,20},{20,16},{24,28},{28,24},{1,5},{5... | collective-permute-start | bytes 663560 | tf_op jit(solution)/shard_map/ppermute | solution.py:360
  387.9 6.6 %collective-permute-done.22 = bf16[192,1024]{1,0:T(8,128)(2,1)S(1)} collective-permute-done((bf16[192,1024]{1,0:T(8,128)(2,1)S(1)}, bf16[192,1024]{1,0:T(8,128)(2,1)S(1)}, u32[]{:S(2)}, u32[]{:S(2)}) %collective-permute-start.22) | collective-permute-done | bytes 393248 | tf_op jit(solution)/shard_map/ppermute | solution.py:357
  (247 shorter events, 108.5 us)
Async XLA Ops:
  6.2 23.9 %collective-permute-start.15 = (bf16[3,96,192]{2,1,0:T(8,128)(2,1)}, bf16[3,96,192]{2,1,0:T(8,128)(2,1)}, u32[]{:S(2)}, u32[]{:S(2)}) collective-permute-start(bf16[3,96,192]{2,1,0:T(8,128)(2,1)} %constant_dynamic-slice_fusion.2), channel_id=1, source_target_pairs={{0,3},{1,0},{2,1},{3,2},{4,7},{5,4},{6,5},{7,6},{8,11},{9,8},{10,9... | collective-permute-start | bytes 331784 | tf_op jit(solution)/shard_map/ppermute | solution.py:352
  6.4 25.9 %collective-permute-start.16 = (bf16[3,96,192]{2,1,0:T(8,128)(2,1)}, bf16[3,96,192]{2,1,0:T(8,128)(2,1)}, u32[]{:S(2)}, u32[]{:S(2)}) collective-permute-start(bf16[3,96,192]{2,1,0:T(8,128)(2,1)} %constant_dynamic-slice_fusion.2), channel_id=1, source_target_pairs={{0,2},{1,3},{2,0},{3,1},{4,6},{5,7},{6,4},{7,5},{8,10},{9,11},{10,... | collective-permute-start | bytes 331784 | tf_op jit(solution)/shard_map/ppermute | solution.py:352
  8.7 23.7 %collective-permute-start.17 = (bf16[3,96,192]{2,1,0:T(8,128)(2,1)}, bf16[3,96,192]{2,1,0:T(8,128)(2,1)}, u32[]{:S(2)}, u32[]{:S(2)}) collective-permute-start(bf16[3,96,192]{2,1,0:T(8,128)(2,1)} %constant_dynamic-slice_fusion.2), channel_id=1, source_target_pairs={{0,1},{1,2},{2,3},{3,0},{4,5},{5,6},{6,7},{7,4},{8,9},{9,10},{10,1... | collective-permute-start | bytes 331784 | tf_op jit(solution)/shard_map/ppermute | solution.py:352
  11.6 40.4 %collective-permute-start.3 = (bf16[3,24,192]{2,1,0:T(8,128)(2,1)}, bf16[3,24,192]{2,1,0:T(8,128)(2,1)}, u32[]{:S(2)}, u32[]{:S(2)}) collective-permute-start(bf16[3,24,192]{2,1,0:T(8,128)(2,1)} %constant_dynamic-slice_fusion.7), channel_id=1, source_target_pairs={{0,3},{1,0},{2,1},{3,2},{4,7},{5,4},{6,5},{7,6},{8,11},{9,8},{10,9... | collective-permute-start | bytes 82952 | tf_op jit(solution)/shard_map/ppermute | solution.py:352
  11.6 40.4 %collective-permute-start.4 = (bf16[3,24,192]{2,1,0:T(8,128)(2,1)}, bf16[3,24,192]{2,1,0:T(8,128)(2,1)}, u32[]{:S(2)}, u32[]{:S(2)}) collective-permute-start(bf16[3,24,192]{2,1,0:T(8,128)(2,1)} %constant_dynamic-slice_fusion.7), channel_id=1, source_target_pairs={{0,2},{1,3},{2,0},{3,1},{4,6},{5,7},{6,4},{7,5},{8,10},{9,11},{10,... | collective-permute-start | bytes 82952 | tf_op jit(solution)/shard_map/ppermute | solution.py:352
  30.1 22.4 %collective-permute-start.5 = (bf16[3,24,192]{2,1,0:T(8,128)(2,1)}, bf16[3,24,192]{2,1,0:T(8,128)(2,1)S(1)}, u32[]{:S(2)}, u32[]{:S(2)}) collective-permute-start(bf16[3,24,192]{2,1,0:T(8,128)(2,1)} %constant_dynamic-slice_fusion.7), channel_id=1, source_target_pairs={{0,1},{1,2},{2,3},{3,0},{4,5},{5,6},{6,7},{7,4},{8,9},{9,10},{10,1... | collective-permute-start | bytes 82952 | tf_op jit(solution)/shard_map/ppermute | solution.py:352
  32.3 16.1 %collective-permute-start.11 = (f32[13,192]{0,1:T(8,128)}, f32[13,192]{0,1:T(8,128)S(1)}, u32[]{:S(2)}, u32[]{:S(2)}) collective-permute-start(f32[13,192]{0,1:T(8,128)} %copy.116), channel_id=1, source_target_pairs={{0,1},{1,2},{2,3},{3,0},{4,5},{5,6},{6,7},{7,4},{8,9},{9,10},{10,1... | collective-permute-start | bytes 29960 | tf_op jit(solution)/shard_map/ppermute | solution.py:352
  46.7 17.1 %collective-permute-start.19 = (bf16[3,3,192,192]{3,2,1,0:T(8,128)(2,1)S(1)}, bf16[3,3,192,192]{3,2,1,0:T(8,128)(2,1)S(1)}, u32[]{:S(2)}, u32[]{:S(2)}) collective-permute-start(bf16[3,3,192,192]{3,2,1,0:T(8,128)(2,1)S(1)} %maximum_select_fusion.4), channel_id=1, source_target_pairs={{0,8},{4,12},{8,0},{12,4},{16,24},{20,28},{24,16},{28,20},{1,9},{5... | collective-permute-start | bytes 1990664 | tf_op jit(solution)/shard_map/ppermute | solution.py:360
  48.3 25.9 %collective-permute-start.10 = (f32[13,192]{0,1:T(8,128)S(1)}, f32[13,192]{0,1:T(8,128)S(1)}, u32[]{:S(2)}, u32[]{:S(2)}) collective-permute-start(f32[13,192]{0,1:T(8,128)S(1)} %copy-done.26), channel_id=1, source_target_pairs={{0,2},{1,3},{2,0},{3,1},{4,6},{5,7},{6,4},{7,5},{8,10},{9,11},{10,... | collective-permute-start | bytes 29960 | tf_op jit(solution)/shard_map/ppermute | solution.py:352
  52.0 46.6 %collective-permute-start.1 = (bf16[192,1024]{1,0:T(8,128)(2,1)}, bf16[192,1024]{1,0:T(8,128)(2,1)S(1)}, u32[]{:S(2)}, u32[]{:S(2)}) collective-permute-start(bf16[192,1024]{1,0:T(8,128)(2,1)} %get-tuple-element.117), channel_id=1, source_target_pairs={{0,2},{1,3},{2,0},{3,1},{4,6},{5,7},{6,4},{7,5},{8,10},{9,11},{10,... | collective-permute-start | bytes 1179656 | tf_op jit(solution)/shard_map/ppermute | solution.py:352
  52.1 59.8 %collective-permute-start.2 = (bf16[192,1024]{1,0:T(8,128)(2,1)}, bf16[192,1024]{1,0:T(8,128)(2,1)S(1)}, u32[]{:S(2)}, u32[]{:S(2)}) collective-permute-start(bf16[192,1024]{1,0:T(8,128)(2,1)} %get-tuple-element.114), channel_id=1, source_target_pairs={{0,1},{1,2},{2,3},{3,0},{4,5},{5,6},{6,7},{7,4},{8,9},{9,10},{10,1... | collective-permute-start | bytes 1179656 | tf_op jit(solution)/shard_map/ppermute | solution.py:352
  53.4 18.0 %collective-permute-start.6 = (bf16[3,3,24,192]{3,2,1,0:T(8,128)(2,1)S(1)}, bf16[3,3,24,192]{3,2,1,0:T(8,128)(2,1)S(1)}, u32[]{:S(2)}, u32[]{:S(2)}) collective-permute-start(bf16[3,3,24,192]{3,2,1,0:T(8,128)(2,1)S(1)} %pad_maximum_fusion.5), channel_id=1, source_target_pairs={{0,16},{4,20},{8,24},{12,28},{16,0},{20,4},{24,8},{28,12},{1,17},{... | collective-permute-start | bytes 248840 | tf_op jit(solution)/shard_map/ppermute | solution.py:360
  66.4 71.7 %collective-permute-start.20 = (bf16[3,3,384,192]{2,3,1,0:T(8,128)(2,1)}, bf16[3,3,384,192]{2,3,1,0:T(8,128)(2,1)}, u32[]{:S(2)}, u32[]{:S(2)}) collective-permute-start(bf16[3,3,384,192]{2,3,1,0:T(8,128)(2,1)} %copy.128), channel_id=1, source_target_pairs={{0,4},{4,0},{8,12},{12,8},{16,20},{20,16},{24,28},{28,24},{1,5},{5... | collective-permute-start | bytes 3981320 | tf_op jit(solution)/shard_map/ppermute | solution.py:360
  72.0 52.9 %collective-permute-start = (bf16[192,1024]{1,0:T(8,128)(2,1)}, bf16[192,1024]{1,0:T(8,128)(2,1)S(1)}, u32[]{:S(2)}, u32[]{:S(2)}) collective-permute-start(bf16[192,1024]{1,0:T(8,128)(2,1)} %get-tuple-element.115), channel_id=1, source_target_pairs={{0,3},{1,0},{2,1},{3,2},{4,7},{5,4},{6,5},{7,6},{8,11},{9,8},{10,9... | collective-permute-start | bytes 1179656 | tf_op jit(solution)/shard_map/ppermute | solution.py:352
  92.9 52.2 %collective-permute-start.12 = (bf16[192,1024]{1,0:T(8,128)(2,1)}, bf16[192,1024]{1,0:T(8,128)(2,1)}, u32[]{:S(2)}, u32[]{:S(2)}) collective-permute-start(bf16[192,1024]{1,0:T(8,128)(2,1)} %get-tuple-element.112), channel_id=1, source_target_pairs={{0,3},{1,0},{2,1},{3,2},{4,7},{5,4},{6,5},{7,6},{8,11},{9,8},{10,9... | collective-permute-start | bytes 1179656 | tf_op jit(solution)/shard_map/ppermute | solution.py:352
  98.7 46.4 %collective-permute-start.13 = (bf16[192,1024]{1,0:T(8,128)(2,1)}, bf16[192,1024]{1,0:T(8,128)(2,1)}, u32[]{:S(2)}, u32[]{:S(2)}) collective-permute-start(bf16[192,1024]{1,0:T(8,128)(2,1)} %get-tuple-element.111), channel_id=1, source_target_pairs={{0,2},{1,3},{2,0},{3,1},{4,6},{5,7},{6,4},{7,5},{8,10},{9,11},{10,... | collective-permute-start | bytes 1179656 | tf_op jit(solution)/shard_map/ppermute | solution.py:352
  111.9 33.2 %collective-permute-start.14 = (bf16[192,1024]{1,0:T(8,128)(2,1)}, bf16[192,1024]{1,0:T(8,128)(2,1)}, u32[]{:S(2)}, u32[]{:S(2)}) collective-permute-start(bf16[192,1024]{1,0:T(8,128)(2,1)} %get-tuple-element.110), channel_id=1, source_target_pairs={{0,1},{1,2},{2,3},{3,0},{4,5},{5,6},{6,7},{7,4},{8,9},{9,10},{10,1... | collective-permute-start | bytes 1179656 | tf_op jit(solution)/shard_map/ppermute | solution.py:352
  190.7 77.0 %collective-permute-start.39 = (bf16[4,1152,192]{1,2,0:T(8,128)(2,1)}, bf16[4,1152,192]{1,2,0:T(8,128)(2,1)}, u32[]{:S(2)}, u32[]{:S(2)}) collective-permute-start(bf16[4,1152,192]{1,2,0:T(8,128)(2,1)} %copy.143), channel_id=1, source_target_pairs={{0,4},{4,0},{8,12},{12,8},{16,20},{20,16},{24,28},{28,24},{1,5},{5... | collective-permute-start | bytes 5308424 | tf_op jit(solution)/shard_map/ppermute | solution.py:360
  259.4 16.5 %collective-permute-start.36 = (f32[12,192]{0,1:T(8,128)S(1)}, f32[12,192]{0,1:T(8,128)S(1)}, u32[]{:S(2)}, u32[]{:S(2)}) collective-permute-start(f32[12,192]{0,1:T(8,128)S(1)} %get-tuple-element.123), channel_id=1, source_target_pairs={{0,1},{1,2},{2,3},{3,0},{4,5},{5,6},{6,7},{7,4},{8,9},{9,10},{10,1... | collective-permute-start | bytes 27656 | tf_op jit(solution)/shard_map/ppermute | solution.py:357
  260.9 15.4 %collective-permute-start.37 = (f32[12,192]{0,1:T(8,128)S(1)}, f32[12,192]{0,1:T(8,128)S(1)}, u32[]{:S(2)}, u32[]{:S(2)}) collective-permute-start(f32[12,192]{0,1:T(8,128)S(1)} %get-tuple-element.125), channel_id=1, source_target_pairs={{0,2},{1,3},{2,0},{3,1},{4,6},{5,7},{6,4},{7,5},{8,10},{9,11},{10,... | collective-permute-start | bytes 27656 | tf_op jit(solution)/shard_map/ppermute | solution.py:357
  262.3 14.9 %collective-permute-start.38 = (f32[12,192]{0,1:T(8,128)S(1)}, f32[12,192]{0,1:T(8,128)S(1)}, u32[]{:S(2)}, u32[]{:S(2)}) collective-permute-start(f32[12,192]{0,1:T(8,128)S(1)} %get-tuple-element.124), channel_id=1, source_target_pairs={{0,3},{1,0},{2,1},{3,2},{4,7},{5,4},{6,5},{7,6},{8,11},{9,8},{10,9... | collective-permute-start | bytes 27656 | tf_op jit(solution)/shard_map/ppermute | solution.py:357
  265.2 54.4 %collective-permute-start.27 = (bf16[4,288,192]{2,1,0:T(8,128)(2,1)}, bf16[4,288,192]{2,1,0:T(8,128)(2,1)}, u32[]{:S(2)}, u32[]{:S(2)}) collective-permute-start(bf16[4,288,192]{2,1,0:T(8,128)(2,1)} %dynamic-slice_convert_fusion.2), channel_id=1, source_target_pairs={{0,4},{4,0},{8,12},{12,8},{16,20},{20,16},{24,28},{28,24},{1,5},{5... | collective-permute-start | bytes 1327112 | tf_op jit(solution)/shard_map/ppermute | solution.py:360
  268.8 95.1 %collective-permute-start.26 = (bf16[192,1024]{1,0:T(8,128)(2,1)}, bf16[192,1024]{1,0:T(8,128)(2,1)}, u32[]{:S(2)}, u32[]{:S(2)}) collective-permute-start(bf16[192,1024]{1,0:T(8,128)(2,1)} %get-tuple-element.90), channel_id=1, source_target_pairs={{0,3},{1,0},{2,1},{3,2},{4,7},{5,4},{6,5},{7,6},{8,11},{9,8},{10,9... | collective-permute-start | bytes 1179656 | tf_op jit(solution)/shard_map/ppermute | solution.py:357
  276.0 48.9 %collective-permute-start.25 = (bf16[192,1024]{1,0:T(8,128)(2,1)}, bf16[192,1024]{1,0:T(8,128)(2,1)}, u32[]{:S(2)}, u32[]{:S(2)}) collective-permute-start(bf16[192,1024]{1,0:T(8,128)(2,1)} %get-tuple-element.84), channel_id=1, source_target_pairs={{0,2},{1,3},{2,0},{3,1},{4,6},{5,7},{6,4},{7,5},{8,10},{9,11},{10,... | collective-permute-start | bytes 1179656 | tf_op jit(solution)/shard_map/ppermute | solution.py:357
  276.4 47.0 %collective-permute-start.24 = (bf16[192,1024]{1,0:T(8,128)(2,1)}, bf16[192,1024]{1,0:T(8,128)(2,1)}, u32[]{:S(2)}, u32[]{:S(2)}) collective-permute-start(bf16[192,1024]{1,0:T(8,128)(2,1)} %get-tuple-element.78), channel_id=1, source_target_pairs={{0,1},{1,2},{2,3},{3,0},{4,5},{5,6},{6,7},{7,4},{8,9},{9,10},{10,1... | collective-permute-start | bytes 1179656 | tf_op jit(solution)/shard_map/ppermute | solution.py:357
  277.2 45.2 %collective-permute-start.40 = (bf16[4,576,192]{1,2,0:T(8,128)(2,1)}, bf16[4,576,192]{1,2,0:T(8,128)(2,1)S(1)}, u32[]{:S(2)}, u32[]{:S(2)}) collective-permute-start(bf16[4,576,192]{1,2,0:T(8,128)(2,1)} %dynamic-slice_convert_fusion), channel_id=1, source_target_pairs={{0,8},{4,12},{8,0},{12,4},{16,24},{20,28},{24,16},{28,20},{1,9},{5... | collective-permute-start | bytes 2654216 | tf_op jit(solution)/shard_map/ppermute | solution.py:360
  319.6 59.8 %collective-permute-start.21 = (bf16[192,1024]{1,0:T(8,128)(2,1)}, bf16[192,1024]{1,0:T(8,128)(2,1)S(1)}, u32[]{:S(2)}, u32[]{:S(2)}) collective-permute-start(bf16[192,1024]{1,0:T(8,128)(2,1)} %get-tuple-element.64), channel_id=1, source_target_pairs={{0,1},{1,2},{2,3},{3,0},{4,5},{5,6},{6,7},{7,4},{8,9},{9,10},{10,1... | collective-permute-start | bytes 1179656 | tf_op jit(solution)/shard_map/ppermute | solution.py:357
  358.5 15.4 %collective-permute-start.46 = (f32[576,192]{0,1:T(8,128)S(1)}, f32[576,192]{0,1:T(8,128)S(1)}, u32[]{:S(2)}, u32[]{:S(2)}) collective-permute-start(f32[576,192]{0,1:T(8,128)S(1)} %maximum_select_fusion.7), channel_id=1, source_target_pairs={{0,8},{4,12},{8,0},{12,4},{16,24},{20,28},{24,16},{28,20},{1,9},{5... | collective-permute-start | bytes 1327112 | tf_op jit(solution)/shard_map/ppermute | solution.py:360
  366.8 27.7 %collective-permute-start.22 = (bf16[192,1024]{1,0:T(8,128)(2,1)S(1)}, bf16[192,1024]{1,0:T(8,128)(2,1)S(1)}, u32[]{:S(2)}, u32[]{:S(2)}) collective-permute-start(bf16[192,1024]{1,0:T(8,128)(2,1)S(1)} %copy-done.38), channel_id=1, source_target_pairs={{0,2},{1,3},{2,0},{3,1},{4,6},{5,7},{6,4},{7,5},{8,10},{9,11},{10,... | collective-permute-start | bytes 1179656 | tf_op jit(solution)/shard_map/ppermute | solution.py:357
  368.6 27.5 %collective-permute-start.23 = (bf16[192,1024]{1,0:T(8,128)(2,1)S(1)}, bf16[192,1024]{1,0:T(8,128)(2,1)S(1)}, u32[]{:S(2)}, u32[]{:S(2)}) collective-permute-start(bf16[192,1024]{1,0:T(8,128)(2,1)S(1)} %copy-done.37), channel_id=1, source_target_pairs={{0,3},{1,0},{2,1},{3,2},{4,7},{5,4},{6,5},{7,6},{8,11},{9,8},{10,9... | collective-permute-start | bytes 1179656 | tf_op jit(solution)/shard_map/ppermute | solution.py:357
  374.2 23.0 %collective-permute-start.47 = (f32[1152,192]{0,1:T(8,128)S(1)}, f32[1152,192]{0,1:T(8,128)S(1)}, u32[]{:S(2)}, u32[]{:S(2)}) collective-permute-start(f32[1152,192]{0,1:T(8,128)S(1)} %maximum_select_fusion.5), channel_id=1, source_target_pairs={{0,4},{4,0},{8,12},{12,8},{16,20},{20,16},{24,28},{28,24},{1,5},{5... | collective-permute-start | bytes 2654216 | tf_op jit(solution)/shard_map/ppermute | solution.py:360
  383.5 12.7 %collective-permute-start.35 = (f32[288,192]{1,0:T(8,128)S(1)}, f32[288,192]{1,0:T(8,128)S(1)}, u32[]{:S(2)}, u32[]{:S(2)}) collective-permute-start(f32[288,192]{1,0:T(8,128)S(1)} %maximum_select_fusion.9), channel_id=1, source_target_pairs={{0,4},{4,0},{8,12},{12,8},{16,20},{20,16},{24,28},{28,24},{1,5},{5... | collective-permute-start | bytes 663560 | tf_op jit(solution)/shard_map/ppermute | solution.py:360
  (55 other events, 444.3 us)
